TPU v7x, 128 devices: a whole 4x4x4 slice. The times are simulated.
128 devices in a mesh: ctx: 16 (over x_lo, z, core), mp: 4 (over y), rep: 2 (over x_hi).
Axes of the slice: x: 4 (x_hi: 2, x_lo: 2; x = x_hi * 2 + x_lo), y: 4, z: 4, core: 2. Of those that a mesh axis runs over, the one named last changes fastest.
Arguments:
- token_pages: bfloat16 [128, 128, 2048], P('ctx'), may hold values from -13 to 13
- page_table: int32 [128], P('ctx'), may hold values from 0 to 7, as said below
- live_flags: int32 [128], P('ctx'), may hold values from 0 to 1, as said below
- lengths: int32 [32], replicated, may hold values from 1 to 1024, as said below
- decay_floor: float32 [2048], P(('mp', 'rep')), may hold values from 0.85 to 0.9998
- mixer_gain: float32 [2048], replicated, may hold values from 0.5 to 1.5
- feed_gain: float32 [2048], replicated, may hold values from 0.5 to 1.5
- trainer_mixer_in: float32 [3, 2048, 2048], P(None, ('ctx', 'mp')), may hold values from -0.125 to 0.125
- trainer_mixer_out: float32 [2048, 2048], P(None, ('ctx', 'mp')), may hold values from -0.125 to 0.125
- trainer_gate_up: float32 [2, 2048, 5632], P(None, ('ctx', 'mp')), may hold values from -0.125 to 0.125
- trainer_down: float32 [5632, 2048], P(None, ('ctx', 'mp')), may hold values from -0.078125 to 0.078125
Outputs:
- layer_output: bfloat16 [16384, 2048], P(('ctx', 'rep'), 'mp')
Inputs may be any that keep to these rules, and one draw needn't show every extreme that they name: `page_table`: within each device's block of 8 entries every value 0 to 7 appears once. `live_flags`: in each device's block of 8 flags at least half (rounded down, and never fewer than one) are ones, and some device's block is all ones. The lengths sum to 128 times the number of ones in live_flags; one prompt has exactly 1024 tokens.
All inputs are finite; a program needn't handle non-finite values.
Results may differ from a plain program's by a relative error of at most 0.015.
Values may be sent and summed in bfloat16 or wider, within the bound.
A program may use at most 192 MiB of HBM per device.

v0:
```python
import jax
import jax.numpy as jnp
from jax import lax
from jax.sharding import PartitionSpec as P

D = 2048
HEADS = 16
norm_eps = 1e-05


def prefix(value, axis, join, neutral):
    count, mine = (lax.axis_size(axis), lax.axis_index(axis))
    pieces = lax.all_gather(value, axis)
    total = jnp.full_like(value, 0) + jnp.asarray(neutral, value.dtype)

    def prefix_step(position, total):
        longer = join(total, pieces[position])
        return jnp.where(position < mine, longer, total)

    return lax.fori_loop(0, count - 1, prefix_step, total)


def entering_2(shard, axis, combine, identity):
    peers, position = (lax.axis_size(axis), lax.axis_index(axis))
    everything = jax.tree.map(
        lambda part, kind: lax.all_gather(part.astype(kind), axis),
        shard,
        (jnp.bfloat16, jnp.bfloat16),
    )
    start = jax.tree.map(
        lambda part, zero: jnp.broadcast_to(jnp.asarray(zero, part.dtype), part.shape),
        shard,
        identity,
    )

    def entering_step(k, before):
        reached = k < position
        new = combine(
            before, jax.tree.map(lambda part, own: part[k].astype(own.dtype), everything, shard)
        )
        return jax.tree.map(lambda a, b: jnp.where(reached, a, b), new, before)

    return lax.fori_loop(0, peers, entering_step, start)


def rms_scale(values_in, gain):
    mean_sq = jnp.mean(values_in * values_in, axis=-1, keepdims=True)
    return values_in * lax.rsqrt(mean_sq + norm_eps) * gain


def block_recurrence(queries, keys_in, values_in, log_decay, reset_count, state_init, count_init):
    highest = lax.Precision.HIGHEST

    def advance(carried_in, block_data):
        state, count_before = carried_in
        q_block, k_block, v_block, decay_block, count_block = block_data
        cumulative = jnp.cumsum(decay_block, axis=0)
        q_scaled = q_block * jnp.exp(cumulative)
        k_scaled = k_block * jnp.exp(-cumulative)
        scores = jnp.einsum("thd,shd->hts", q_scaled, k_scaled, precision=highest)
        positions = jnp.arange(count_block.shape[0])
        allowed = (positions[:, None] >= positions[None, :]) & (
            count_block[:, None] == count_block[None, :]
        )
        scores = jnp.where(allowed[None], scores, 0.0)
        outputs = jnp.einsum("hts,shd->thd", scores, v_block, precision=highest)
        from_state = jnp.einsum("thd,hde->the", q_scaled, state, precision=highest)
        outputs = outputs + jnp.where((count_block == count_before)[:, None, None], from_state, 0.0)
        last_count = count_block[-1]
        final_cum = cumulative[-1]
        weight_keys = (
            k_block
            * jnp.exp(final_cum[None] - cumulative)
            * (count_block == last_count).astype(k_block.dtype)[:, None, None]
        )
        retained = jnp.where(
            last_count == count_before, jnp.exp(final_cum)[:, :, None] * state, 0.0
        )
        state_next = retained + jnp.einsum("thd,the->hde", weight_keys, v_block, precision=highest)
        return ((state_next, last_count), outputs)

    final_carry, outputs_all = lax.scan(
        advance, (state_init, count_init), (queries, keys_in, values_in, log_decay, reset_count)
    )
    return (outputs_all, final_carry[0])


def compose_states(earlier, later):
    return (earlier[0] * later[0], later[0][:, :, None] * earlier[1] + later[1])


def add_counts(earlier, later):
    return earlier + later


def shards(
    token_pages,
    page_table,
    live_flags,
    lengths,
    decay_floor,
    mixer_gain,
    feed_gain,
    trainer_mixer_in,
    trainer_mixer_out,
    trainer_gate_up,
    trainer_down,
):
    mp_count = lax.axis_size("mp")
    rep_count = lax.axis_size("rep")
    mp_index = lax.axis_index("mp")
    rep_index = lax.axis_index("rep")
    width_local = trainer_mixer_in.shape[1]
    model_width = trainer_mixer_in.shape[2]
    head_cols = decay_floor.shape[0]
    head_dim = D // HEADS
    local_heads = head_cols // head_dim
    hidden_block = trainer_gate_up.shape[2] // mp_count
    mixer_in = lax.dynamic_index_in_dim(
        trainer_mixer_in.reshape(3, width_local, mp_count, rep_count, head_cols),
        rep_index,
        3,
        keepdims=False,
    )
    mixer_in = jnp.transpose(mixer_in, (1, 2, 0, 3)).reshape(width_local, mp_count, 3 * head_cols)
    mixer_out = lax.dynamic_index_in_dim(
        trainer_mixer_out.reshape(mp_count, rep_count, head_cols, width_local),
        rep_index,
        1,
        keepdims=False,
    )
    mixer_out = jnp.transpose(mixer_out, (2, 0, 1))
    gate_up = trainer_gate_up.reshape(2, width_local, mp_count, hidden_block)
    down_rows = trainer_down.reshape(mp_count, hidden_block, width_local)
    gate_up = jnp.transpose(gate_up, (1, 2, 0, 3)).reshape(width_local, mp_count, 2 * hidden_block)
    down_rows = jnp.transpose(down_rows, (2, 0, 1))
    packed = jnp.concatenate([mixer_in, mixer_out, gate_up, down_rows], axis=2).astype(jnp.bfloat16)
    arrived = lax.all_to_all(packed, "mp", split_axis=1, concat_axis=0, tiled=True)
    arrived = arrived.reshape(mp_count * width_local, packed.shape[2])
    served = lax.all_gather(arrived, "ctx", axis=0, tiled=True)
    w_mixer = served[:, : 3 * head_cols]
    w_output_t = served[:, 3 * head_cols : 4 * head_cols]
    feed_weights = served[:, 4 * head_cols :].reshape(model_width, 3, hidden_block)
    pages_local = token_pages.shape[0]
    page_len = token_pages.shape[1]
    tok_count = pages_local * page_len
    ordered = jnp.take(token_pages, page_table, axis=0).reshape(tok_count, model_width)
    live_tokens = jnp.repeat(live_flags, page_len)
    page_live = live_flags * page_len
    live_total = jnp.sum(page_live)
    stream_base = prefix(live_total, "ctx", add_counts, jnp.zeros((), jnp.int32))
    page_start = stream_base + jnp.cumsum(page_live) - page_live
    positions = (page_start[:, None] + jnp.arange(page_len, dtype=jnp.int32)[None, :]).reshape(
        tok_count
    )
    starts = jnp.cumsum(lengths) - lengths
    resets = (live_tokens == 1) & jnp.any(positions[:, None] == starts[None, :], axis=1)
    reset_count = jnp.cumsum(resets.astype(jnp.int32))
    live_float = live_tokens.astype(jnp.float32)[:, None]
    normed = rms_scale(ordered.astype(jnp.float32), mixer_gain).astype(jnp.bfloat16)
    projected = jnp.dot(normed, w_mixer, preferred_element_type=jnp.float32).reshape(
        tok_count, 3, head_cols
    )
    queries = jax.nn.silu(projected[:, 0])
    forget = decay_floor + (1.0 - decay_floor) * jax.nn.sigmoid(projected[:, 1])
    log_decay = jnp.log(forget) * live_float
    keys_in = (1.0 - forget) * live_float
    values_in = projected[:, 2]
    shape_blocks = (pages_local, page_len, local_heads, head_dim)
    local_out, local_state = block_recurrence(
        queries.reshape(shape_blocks),
        keys_in.reshape(shape_blocks),
        values_in.reshape(shape_blocks),
        log_decay.reshape(shape_blocks),
        reset_count.reshape(pages_local, page_len),
        jnp.zeros((local_heads, head_dim, head_dim), jnp.float32),
        jnp.zeros((), jnp.int32),
    )
    device_decay = jnp.where(
        reset_count[-1] == 0, jnp.exp(jnp.sum(log_decay, axis=0)), 0.0
    ).reshape(local_heads, head_dim)
    identity = (
        jnp.ones((local_heads, head_dim), jnp.float32),
        jnp.zeros((local_heads, head_dim, head_dim), jnp.float32),
    )
    entering = entering_2((device_decay, local_state), "ctx", compose_states, identity)[1]
    cum_device = jnp.cumsum(log_decay, axis=0).reshape(tok_count, local_heads, head_dim)
    scaled_queries = queries.reshape(tok_count, local_heads, head_dim) * jnp.exp(cum_device)
    correction = jnp.einsum(
        "thd,hde->the", scaled_queries, entering, precision=lax.Precision.HIGHEST
    )
    mixed = local_out.reshape(tok_count, local_heads, head_dim) + jnp.where(
        (reset_count == 0)[:, None, None], correction, 0.0
    )
    head_normed = (
        (mixed * lax.rsqrt(jnp.mean(mixed * mixed, axis=-1, keepdims=True) + norm_eps))
        .reshape(tok_count, head_cols)
        .astype(jnp.bfloat16)
    )
    half_rows = tok_count // rep_count
    col_block = model_width // mp_count
    attn_term = lax.dot_general(
        head_normed, w_output_t, (((1,), (1,)), ((), ())), preferred_element_type=jnp.float32
    )
    attn_all = lax.psum(attn_term.astype(jnp.bfloat16), ("mp", "rep")).astype(jnp.float32)
    residual = lax.dynamic_slice_in_dim(ordered, rep_index * half_rows, half_rows, 0).astype(
        jnp.float32
    ) + lax.dynamic_slice_in_dim(attn_all, rep_index * half_rows, half_rows, 0)
    feed_in = rms_scale(residual, feed_gain).astype(jnp.bfloat16)
    gated = jnp.einsum(
        "td,dcf->tcf", feed_in, feed_weights[:, :2], preferred_element_type=jnp.float32
    )
    hidden = (jax.nn.silu(gated[:, 0]) * gated[:, 1]).astype(jnp.bfloat16)
    down_term = lax.dot_general(
        hidden, feed_weights[:, 2], (((1,), (1,)), ((), ())), preferred_element_type=jnp.float32
    )
    summed = lax.psum_scatter(
        down_term.astype(jnp.bfloat16), "mp", scatter_dimension=1, tiled=True
    ).astype(jnp.float32)
    summed = summed + lax.dynamic_slice_in_dim(residual, mp_index * col_block, col_block, 1)
    live_half = lax.dynamic_slice_in_dim(live_tokens, rep_index * half_rows, half_rows, 0)
    return jnp.where(live_half[:, None] == 1, summed, 0.0).astype(jnp.bfloat16)


def solution(mesh):
    in_specs = (
        P("ctx", None, None),
        P("ctx"),
        P("ctx"),
        P(),
        P(("mp", "rep")),
        P(),
        P(),
        P(None, ("ctx", "mp"), None),
        P(None, ("ctx", "mp")),
        P(None, ("ctx", "mp"), None),
        P(None, ("ctx", "mp")),
    )
    out_specs = P(("ctx", "rep"), "mp")
    return jax.shard_map(shards, mesh=mesh, in_specs=in_specs, out_specs=out_specs, check_vma=False)
```

profile of v0, /device:TPU:1, one launch (start us, length us, event | category | flops | bytes accessed | tf_op | source)
XLA Modules:
  0.0 575.1 jit_solution(12584117254873081062)
XLA Ops:
  6.5 1.4 reshape.427
  12.5 22.0 %all_to_all.15 = bf16[32,4,5248]{2,0,1:T(8,128)(2,1)} all-to-all(bf16[32,4,5248]{2,0,1:T(8,128)(2,1)S(1)} %pad_maximum_fusion), channel_id=1, replica_groups=mesh['ctx'=16,'mp'=4,'rep'=2] {'mp'}, dimensions={1} | all-to-all | bytes 2686976 | tf_op jit(solution)/shard_map/all_to_all | solution.py:138
  36.3 1.3 dynamic-update-slice
  37.6 13.0 %all-reduce = s32[16]{0:T(128)S(1)} all-reduce(s32[16]{0:T(128)S(1)} %dynamic-update-slice), channel_id=1, replica_groups=mesh['ctx'=16,'mp'=4,'rep'=2] {'ctx'}, use_global_device_ids=true, to_apply=%add | all-reduce | flops 16 | bytes 128
  50.7 18.5 %while.42 = (s32[]{:T(128)}, s32[]{:T(128)}, s32[]{:T(128)}, s32[16]{0:T(128)S(1)}, s32[]{:T(128)}) while((s32[]{:T(128)}, s32[]{:T(128)}, s32[]{:T(128)}, s32[16]{0:T(128)S(1)}, s32[]{:T(128)}) %tuple.96), condition=%wide.region_3.4_spmd, body=%wide.region_2.3_spmd.sunk | while | flops 5 | bytes 107 | solution.py:20
  69.8 5.1 gather_fusion
  75.1 3.6 fusion.21
  78.7 3.3 fusion.23
  82.0 68.7 %all-gather.4.cloned.1.call-done = bf16[2048,5248]{1,0:T(8,128)(2,1)} async-done(((bf16[128,5248]{1,0:T(8,128)(2,1)}), bf16[2048,5248]{1,0:T(8,128)(2,1)}) %all-gather.4.cloned.1.call-update) | async-done | bytes 21495824 | tf_op jit(solution)/shard_map/all_gather | solution.py:140
  150.8 2.1 slice_bitcast_fusion.3
  152.9 3.0 copy.104
  155.8 6.2 %fusion.62 = f32[1024,3,256]{2,0,1:T(8,128)S(1)} fusion(bf16[1024,2048,1]{1,0,2:T(8,128)(2,1)} %bitcast.193, bf16[3,256,2048]{2,1,0:T(8,128)(2,1)} %bitcast.197), kind=kOutput, calls=%fused_computation.127 | convolution fusion | flops 3221225472 | bytes 10485760 | tf_op jit(solution)/shard_map/dot_general | solution.py:161
  162.1 1.7 copy-done.2
  163.7 1.7 fusion.60
  165.4 1.7 div.45
  167.1 1.5 squeeze.62
  168.6 3.3 divide_multiply_fusion
  171.9 2.8 reshape_squeeze.3
  174.7 2.4 subtract_multiply_fusion
  177.1 95.7 %while.43 = (s32[]{:T(128)}, f32[2,128,128]{2,1,0:T(8,128)S(1)}, s32[]{:T(128)}, f32[8,128,2,128]{1,0,3,2:T(8,128)}, s32[8,128]{1,0:T(8,128)S(1)}, /*index=5*/f3...) while((s32[]{:T(128)}, f32[2,128,128]{2,1,0:T(8,128)S(1)}, ...), condition=%wide.region_11.12_spmd.clone, body=%wide.region_9.11_spmd.clone.sunk | while | flops 205996416 | bytes 3712938 | solution.py:82
  179.4 1.2 bitcast_multiply_fusion.5
  182.7 4.8 dynamic_update_slice.6
  191.4 1.2 bitcast_multiply_fusion.5
  194.7 4.8 dynamic_update_slice.6
  203.4 1.2 bitcast_multiply_fusion.5
  206.6 4.8 dynamic_update_slice.6
  215.3 1.2 bitcast_multiply_fusion.5
  218.6 4.8 dynamic_update_slice.6
  230.6 4.8 dynamic_update_slice.6
  242.5 4.8 dynamic_update_slice.6
  254.5 4.8 dynamic_update_slice.6
  266.5 4.8 dynamic_update_slice.6
  275.5 2.4 reshape.434
  277.9 1.7 fusion.58
  280.8 1.4 copy.111
  282.2 18.9 %all_gather.22 = bf16[16,2,128]{2,1,0:T(2,128)(2,1)S(1)} all-gather(bf16[1,2,128]{2,1,0:T(2,128)(2,1)S(1)} %fusion.52), channel_id=1, replica_groups=mesh['ctx'=16,'mp'=4,'rep'=2] {'ctx'}, dimensions={0}, use_global_device_ids=true | all-gather | bytes 8704 | tf_op jit(solution)/shard_map/all_gather | solution.py:26
  301.1 6.1 %all-gather.6.cloned.1.call-done = bf16[32,128,128]{2,1,0:T(8,128)(2,1)} async-done(((bf16[2,128,128]{2,1,0:T(8,128)(2,1)}), bf16[32,128,128]{2,1,0:T(8,128)(2,1)}) %all-gather.6.cloned.1.call-update) | async-done | bytes 1048592 | tf_op jit(solution)/shard_map/all_gather | solution.py:26
  307.2 16.2 %while.44 = (s32[]{:T(128)}, f32[2,128,128]{2,1,0:T(8,128)S(1)}, s32[]{:T(128)}, bf16[16,2,128]{2,1,0:T(2,128)(2,1)S(1)}, bf16[16,2,128,128]{3,2,1,0:T(8,128)(2,1)}, /*index=5*/s32[]{:T(128)}, s32[]{:T(128)}) while((s32[]{:T(128)}, f32[2,128,128]{2,1,0:T(8,128)S(1)}, s32[]{:T(128)}, bf16[16,2,128]{2,1,0:T(2,128)(2,1)S(1)}, ...), condition=%wide.region_14.15_spmd.clone, body=%wide.region_13.14_spmd.clone.sunk | while | flops 164100 | bytes 330345 | solution.py:43
  323.4 2.9 multiply_reduce_fusion.1
  326.4 4.5 convolution_convert_fusion
  331.2 14.2 %slice.81 = bf16[2048,4224]{1,0:T(8,128)(2,1)} slice(bf16[2048,5248]{1,0:T(8,128)(2,1)} %all-gather.4.cloned.1.call-done), slice={[0:2048], [1024:5248]} | slice | bytes 34603008 | tf_op jit(solution)/shard_map/slice | solution.py:143
  345.4 22.6 %copy.114 = bf16[2048,4224]{0,1:T(8,128)(2,1)} copy(bf16[2048,4224]{1,0:T(8,128)(2,1)} %slice.81) | data formatting | bytes 34603008 | tf_op jit(solution)/shard_map/slice | solution.py:143
  368.0 147.3 %all-reduce.3.cloned.1.call-done = bf16[1024,2048]{1,0:T(8,128)(2,1)} async-done(((bf16[1024,2048]{1,0:T(8,128)(2,1)}), bf16[1024,2048]{1,0:T(8,128)(2,1)}) %all-reduce.3.cloned.1.call-update) | async-done | bytes 4194320 | tf_op jit(solution)/shard_map/psum | solution.py:205
  515.3 3.2 multiply_reduce_fusion
  518.5 11.2 %fusion.19 = f32[512,2,1408]{2,0,1:T(8,128)S(1)} fusion(bf16[2048,3,1408]{0,2,1:T(8,128)(2,1)} %bitcast.190, f32[512,2048]{1,0:T(8,128)S(1)} %get-tuple-element.362, f32[2048]{0:T(1024)S(1)} %copy-done.9, f32[512]{0:T(512)S(1)} %add_rsqrt_fusion.2), kind=kOutput, calls=%fused_computation.36 | convolution fusion | flops 5908725760 | bytes 21506048 | tf_op jit(solution)/shard_map/td,dcf->tcf/dot_general | solution.py:210
  529.7 7.3 %fusion.25 = bf16[512,2048]{1,0:T(8,128)(2,1)} fusion(bf16[2048,3,1408]{0,2,1:T(8,128)(2,1)} %bitcast.191, f32[512,2,1408]{2,0,1:T(8,128)S(1)} %fusion.19), kind=kOutput, calls=%fused_computation.51 | convolution fusion | flops 2958163968 | bytes 13631488 | tf_op jit(solution)/shard_map/dot_general | solution.py:214
  537.2 29.1 %reduce-scatter.2.cloned.1.call-done = bf16[512,512]{1,0:T(8,128)(2,1)} async-done(((bf16[512,2048]{1,0:T(8,128)(2,1)}), bf16[512,512]{1,0:T(8,128)(2,1)}) %reduce-scatter.2.cloned.1.call-update) | async-done | bytes 524304 | tf_op jit(solution)/shard_map/reduce_scatter | solution.py:217
  566.3 2.3 select_convert_fusion
  (239 shorter events, 77.5 us)
Async XLA Ops:
  6.5 3.1 copy-start.3
  6.5 144.2 %all-gather.4.cloned.1.call-start = ((), (), s32[]{:S(2)}) async-start(), calls=%async_computation.2 | async-start | bytes 22839296 | tf_op jit(solution)/shard_map/all_gather | solution.py:140
  11.1 23.5 %copy-start.6 = (s32[8]{0:T(128)S(1)}, s32[8]{0:T(128)}, u32[]{:S(2)}) copy-start(s32[8]{0:T(128)} %param.19) | copy-start | bytes 100
  11.1 23.5 %copy-start.8 = (s32[8]{0:T(128)S(1)}, s32[8]{0:T(128)}, u32[]{:S(2)}) copy-start(s32[8]{0:T(128)} %param.18) | copy-start | bytes 100
  11.2 24.3 %copy-start.7 = (s32[32]{0:T(128)S(1)}, s32[32]{0:T(128)}, u32[]{:S(2)}) copy-start(s32[32]{0:T(128)} %param.20) | copy-start | bytes 388
  11.2 24.6 %copy-start.10 = (u32[128]{0:T(128)S(1)}, u32[128]{0:T(128)}, u32[]{:S(2)}) copy-start(u32[128]{0:T(128)} %constant.161) | copy-start | bytes 1540
  34.5 272.6 %all-gather.6.cloned.1.call-start = ((), (), s32[]{:S(2)}) async-start(), calls=%async_computation.5 | async-start | bytes 1114112 | tf_op jit(solution)/shard_map/all_gather | solution.py:26
  69.8 5.2 copy-start.4
  74.9 3.8 copy-start
  74.9 3.8 copy-start.5
  162.1 1.7 copy-start.2
  273.5 241.7 %all-reduce.3.cloned.1.call-start = ((), (), s32[]{:S(2)}) async-start(), calls=%async_computation.3 | async-start | bytes 8388608 | tf_op jit(solution)/shard_map/psum | solution.py:205
  331.0 235.3 %reduce-scatter.2.cloned.1.call-start = ((), (), s32[]{:S(2)}) async-start(), calls=%async_computation.4 | async-start | bytes 2621440 | tf_op jit(solution)/shard_map/reduce_scatter | solution.py:217
  515.3 3.2 copy-start.9
  518.5 11.2 %copy-start.1 = (f32[512,2048]{1,0:T(8,128)}, f32[512,2048]{1,0:T(8,128)S(1)}, u32[]{:S(2)}) copy-start(f32[512,2048]{1,0:T(8,128)S(1)} %get-tuple-element.362) | copy-start | bytes 12582916
Sparse Core Ops, SparseCore 0:
  34.7 116.0 all-gather.3
  273.7 33.4 all-gather.5
  331.1 184.1 all-reduce.2
  537.2 29.0 reduce-scatter.1
where the time goes:
time: 578 us; the launch traced here: 575 us
  waiting for transfers between devices  251 us (43%)
  local copies, waits for them, and re-layouts  127 us (22%)
  other arithmetic  65.4 us (11%)
  blocking collectives  54 us (9%)
  matrix products  42.7 us (7%)
  loops' own time  20.7 us (4%)
  between operations  14.2 us (2%)
    psum x1, waiting for transfers between devices, shards(): lax.psum(attn_term.astype(jnp.bfloat16), ('mp', 'rep')).astype(jnp.float32)  147 us
    all_gather x1, waiting for transfers between devices, shards(): served = lax.all_gather(arrived, 'ctx', axis=0, tiled=True)  68.7 us
    dynamic_update_slice x16, local copies, waits for them, and re-layouts, block_recurrence(): lax.scan(advance, (state_init, count_init), (queries, keys_in, values_in,...  38.8 us
    slice x2, local copies, waits for them, and re-layouts, shards(): served[:, 4 * head_cols:].reshape(model_width, 3, hidden_block)  36.8 us
    reduce_scatter x1, waiting for transfers between devices, shards(): lax.psum_scatter(down_term.astype(jnp.bfloat16), 'mp', scatter_dimension=...  29.1 us
    all_to_all x1, blocking collectives, shards(): lax.all_to_all(packed, 'mp', split_axis=1, concat_axis=0, tiled=True)  22 us
    all_gather x1, blocking collectives, entering_2(): lax.all_gather(part.astype(kind), axis)  18.9 us
    select_n x16, other arithmetic, entering_step(): return jax.tree.map(lambda a, b: jnp.where(reached, a, b), new, before)  15.5 us
  transfers between devices with their start and end apart: 4, of which 4 were waited for; matrix products, arithmetic and copies ran while one was open for 12% of the time, Pallas kernels for 0%

commit v1 on v0

--- a/solution.py
+++ b/solution.py
@@ -137,7 +137,16 @@
     packed = jnp.concatenate([mixer_in, mixer_out, gate_up, down_rows], axis=2).astype(jnp.bfloat16)
     arrived = lax.all_to_all(packed, "mp", split_axis=1, concat_axis=0, tiled=True)
     arrived = arrived.reshape(mp_count * width_local, packed.shape[2])
-    served = lax.all_gather(arrived, "ctx", axis=0, tiled=True)
+    work_table = lambda field: jnp.concatenate(
+        lax.all_to_all(
+            jnp.stack([field for _ in range(lax.axis_size("ctx"))]),
+            axis_name="ctx",
+            split_axis=0,
+            concat_axis=0,
+        ),
+        axis=0,
+    )
+    served = work_table(arrived)
     w_mixer = served[:, : 3 * head_cols]
     w_output_t = served[:, 3 * head_cols : 4 * head_cols]
     feed_weights = served[:, 4 * head_cols :].reshape(model_width, 3, hidden_block)

time: 578 us -> 849 us (1.47)
  blocking collectives: 54 us -> 371 us
  waiting for transfers between devices: 251 us -> 204 us
    unnamed x1, blocking collectives: 13 us -> 332 us
    all_gather x1 -> x0, waiting for transfers between devices: 68.7 us -> none  [shards(): served = lax.all_gather(arrived, 'ctx', axis=0, tiled=True)]
    psum x1, waiting for transfers between devices: 147 us -> 169 us  [shards(): lax.psum(attn_term.astype(jnp.bfloat16), ('mp', 'rep')).astype(jnp.float32)]
    slice x2 -> x1, local copies, waits for them, and re-layouts: 36.8 us -> 14.8 us  [shards(): served[:, 4 * head_cols:].reshape(model_width, 3, hidden_block)]
    reshape x0 -> x1, local copies, waits for them, and re-layouts: none -> 10.8 us  [shards(): jnp.concatenate(lax.all_to_all(jnp.stack([field for _ in range(lax.axis_s...]
    another operation x8 -> x10, local copies, waits for them, and re-layouts: 0.85 us -> 9.51 us  [the longest x2 8.67 us: shards(): jnp.stack([field for _ in range(lax.axis_size('ctx'))])]
  transfers between devices with their start and end apart: 4 -> 4, of which waited for: 4 -> 3; matrix products, arithmetic and copies ran while one was open for 12% -> 6% of each run, Pallas kernels for 0% -> 0%
where the time goes in v1:
time: 849 us; the launch traced here: 846 us
  blocking collectives  371 us (44%)
  waiting for transfers between devices  204 us (24%)
  local copies, waits for them, and re-layouts  123 us (14%)
  other arithmetic  65.2 us (8%)
  matrix products  39.9 us (5%)
  loops' own time  20.3 us (2%)
  between operations  14.3 us (2%)
  starting transfers between devices  8.61 us (1%)
    unnamed x1, blocking collectives  332 us
    psum x1, waiting for transfers between devices, shards(): lax.psum(attn_term.astype(jnp.bfloat16), ('mp', 'rep')).astype(jnp.float32)  169 us
    dynamic_update_slice x16, local copies, waits for them, and re-layouts, block_recurrence(): lax.scan(advance, (state_init, count_init), (queries, keys_in, values_in,...  38.7 us
    reduce_scatter x1, waiting for transfers between devices, shards(): lax.psum_scatter(down_term.astype(jnp.bfloat16), 'mp', scatter_dimension=...  29.1 us
    all_to_all x1, blocking collectives, shards(): lax.all_to_all(packed, 'mp', split_axis=1, concat_axis=0, tiled=True)  21.9 us
    all_gather x1, blocking collectives, entering_2(): lax.all_gather(part.astype(kind), axis)  17.3 us
  transfers between devices with their start and end apart: 4, of which 3 were waited for; matrix products, arithmetic and copies ran while one was open for 6% of the time, Pallas kernels for 0%

profile of v1, /device:TPU:1, one launch (start us, length us, event | category | flops | bytes accessed | tf_op | source)
XLA Modules:
  0.0 846.4 jit_solution(3530348017346799924)
XLA Ops:
  6.5 1.4 reshape.429
  12.4 21.9 %all_to_all.20 = bf16[32,4,5248]{2,0,1:T(8,128)(2,1)S(1)} all-to-all(bf16[32,4,5248]{2,0,1:T(8,128)(2,1)S(1)} %pad_maximum_fusion), channel_id=1, replica_groups=mesh['ctx'=16,'mp'=4,'rep'=2] {'mp'}, dimensions={1} | all-to-all | bytes 2686976 | tf_op jit(solution)/shard_map/all_to_all | solution.py:138
  35.4 7.6 stack.3
  43.0 8.5 %all-to-all-start.1 = ((bf16[16,128,5248]{1,2,0:T(8,128)(2,1)}), bf16[16,128,5248]{1,2,0:T(8,128)(2,1)}, u32[]{:S(2)}, u32[]{:S(2)}) async-start(bf16[16,128,5248]{1,2,0:T(8,128)(2,1)} %stack.3), calls=%async_computation.1 | async-start | bytes 42991616 | tf_op jit(solution)/shard_map/all_to_all | solution.py:141
  53.4 1.4 dynamic-update-slice
  54.7 331.8 %all-reduce = s32[16]{0:T(128)S(1)} all-reduce(s32[16]{0:T(128)S(1)} %dynamic-update-slice), channel_id=1, replica_groups=mesh['ctx'=16,'mp'=4,'rep'=2] {'ctx'}, use_global_device_ids=true, to_apply=%add | all-reduce | flops 16 | bytes 128
  386.5 19.3 %while.42 = (s32[]{:T(128)}, s32[]{:T(128)}, s32[]{:T(128)}, s32[16]{0:T(128)S(1)}, s32[]{:T(128)}) while((s32[]{:T(128)}, s32[]{:T(128)}, s32[]{:T(128)}, s32[16]{0:T(128)S(1)}, s32[]{:T(128)}) %tuple.96), condition=%wide.region_3.4_spmd, body=%wide.region_2.3_spmd.sunk | while | flops 5 | bytes 107 | solution.py:20
  406.5 5.0 gather_fusion
  411.8 3.6 fusion.21
  415.4 3.3 fusion.23
  418.6 10.8 %copy_bitcast_fusion.3 = bf16[2048,5248]{0,1:T(8,128)(2,1)S(1)} fusion(bf16[16,128,5248]{1,2,0:T(8,128)(2,1)} %all-to-all-done.1), kind=kLoop, calls=%fused_computation.36 | loop fusion | bytes 42991616 | tf_op jit(solution)/shard_map/reshape | solution.py:140
  429.8 4.9 copy-done.4
  434.7 3.4 fusion.62
  438.2 1.8 fusion.60
  440.5 1.7 div.45
  442.3 1.5 squeeze.62
  443.8 3.3 divide_multiply_fusion
  447.1 2.8 reshape_squeeze.3
  449.8 2.3 subtract_multiply_fusion
  452.2 94.8 %while.43 = (s32[]{:T(128)}, f32[2,128,128]{2,1,0:T(8,128)S(1)}, s32[]{:T(128)}, f32[8,128,2,128]{1,0,3,2:T(8,128)}, s32[8,128]{1,0:T(8,128)S(1)}, /*index=5*/f3...) while((s32[]{:T(128)}, f32[2,128,128]{2,1,0:T(8,128)S(1)}, ...), condition=%wide.region_11.12_spmd.clone, body=%wide.region_9.11_spmd.clone.sunk | while | flops 205996416 | bytes 3712938 | solution.py:82
  454.4 1.2 bitcast_multiply_fusion.5
  457.7 4.7 dynamic_update_slice.6
  466.2 1.2 bitcast_multiply_fusion.5
  469.5 4.7 dynamic_update_slice.6
  478.1 1.2 bitcast_multiply_fusion.5
  481.4 4.7 dynamic_update_slice.6
  489.9 1.2 bitcast_multiply_fusion.5
  493.2 4.7 dynamic_update_slice.6
  501.8 1.2 bitcast_multiply_fusion.5
  505.1 4.7 dynamic_update_slice.6
  516.9 4.7 dynamic_update_slice.6
  528.7 4.7 dynamic_update_slice.6
  540.6 4.7 dynamic_update_slice.6
  549.4 2.4 reshape.436
  551.8 1.7 fusion.58
  554.7 1.4 copy.110
  556.0 17.3 %all_gather.18 = bf16[16,2,128]{2,1,0:T(2,128)(2,1)S(1)} all-gather(bf16[1,2,128]{2,1,0:T(2,128)(2,1)S(1)} %fusion.52), channel_id=1, replica_groups=mesh['ctx'=16,'mp'=4,'rep'=2] {'ctx'}, dimensions={0}, use_global_device_ids=true | all-gather | bytes 8704 | tf_op jit(solution)/shard_map/all_gather | solution.py:26
  573.3 5.1 all-gather.3.cloned.1.call-done
  578.5 16.2 %while.44 = (s32[]{:T(128)}, f32[2,128,128]{2,1,0:T(8,128)S(1)}, s32[]{:T(128)}, bf16[16,2,128]{2,1,0:T(2,128)(2,1)S(1)}, bf16[16,2,128,128]{3,2,1,0:T(8,128)(2,1)}, /*index=5*/s32[]{:T(128)}, s32[]{:T(128)}) while((s32[]{:T(128)}, f32[2,128,128]{2,1,0:T(8,128)S(1)}, s32[]{:T(128)}, bf16[16,2,128]{2,1,0:T(2,128)(2,1)S(1)}, ...), condition=%wide.region_14.15_spmd.clone, body=%wide.region_13.14_spmd.clone.sunk | while | flops 164100 | bytes 330345 | solution.py:43
  594.7 2.9 multiply_reduce_fusion.1
  597.7 4.5 convolution_convert_fusion
  602.4 14.8 %slice.81 = bf16[2048,4224]{0,1:T(8,128)(2,1)} slice(bf16[2048,5248]{0,1:T(8,128)(2,1)} %copy-done), slice={[0:2048], [1024:5248]} | slice | bytes 34603008 | tf_op jit(solution)/shard_map/slice | solution.py:152
  617.2 169.4 %all-reduce.3.cloned.1.call-done = bf16[1024,2048]{1,0:T(8,128)(2,1)} async-done(((bf16[1024,2048]{1,0:T(8,128)(2,1)}), bf16[1024,2048]{1,0:T(8,128)(2,1)}) %all-reduce.3.cloned.1.call-update) | async-done | bytes 4194320 | tf_op jit(solution)/shard_map/psum | solution.py:214
  786.6 3.2 multiply_reduce_fusion
  789.8 11.2 %fusion.19 = f32[512,2,1408]{2,0,1:T(8,128)S(1)} fusion(bf16[2048,3,1408]{0,2,1:T(8,128)(2,1)} %bitcast.195, f32[512,2048]{1,0:T(8,128)S(1)} %get-tuple-element.362, f32[2048]{0:T(1024)S(1)} %copy-done.11, f32[512]{0:T(512)S(1)} %add_rsqrt_fusion.2), kind=kOutput, calls=%fused_computation.37 | convolution fusion | flops 5908725760 | bytes 21506048 | tf_op jit(solution)/shard_map/td,dcf->tcf/dot_general | solution.py:219
  801.1 7.4 fusion.25
  808.5 29.1 %reduce-scatter.2.cloned.1.call-done = bf16[512,512]{1,0:T(8,128)(2,1)} async-done(((bf16[512,2048]{1,0:T(8,128)(2,1)}), bf16[512,512]{1,0:T(8,128)(2,1)}) %reduce-scatter.2.cloned.1.call-update) | async-done | bytes 524304 | tf_op jit(solution)/shard_map/reduce_scatter | solution.py:226
  837.6 2.3 select_convert_fusion
  (243 shorter events, 78.4 us)
Async XLA Ops:
  6.5 3.1 copy-start.5
  43.0 8.6 %copy-start.8 = (s32[8]{0:T(128)S(1)}, s32[8]{0:T(128)}, u32[]{:S(2)}) copy-start(s32[8]{0:T(128)} %param.19) | copy-start | bytes 100
  43.0 8.6 %copy-start.10 = (s32[8]{0:T(128)S(1)}, s32[8]{0:T(128)}, u32[]{:S(2)}) copy-start(s32[8]{0:T(128)} %param.18) | copy-start | bytes 100
  43.0 9.5 %copy-start.9 = (s32[32]{0:T(128)S(1)}, s32[32]{0:T(128)}, u32[]{:S(2)}) copy-start(s32[32]{0:T(128)} %param.20) | copy-start | bytes 388
  43.0 9.7 %copy-start.12 = (u32[128]{0:T(128)S(1)}, u32[128]{0:T(128)}, u32[]{:S(2)}) copy-start(u32[128]{0:T(128)} %constant.161) | copy-start | bytes 1540
  43.0 375.6 %all-to-all-start.1 = ((bf16[16,128,5248]{1,2,0:T(8,128)(2,1)}), bf16[16,128,5248]{1,2,0:T(8,128)(2,1)}, u32[]{:S(2)}, u32[]{:S(2)}) async-start(bf16[16,128,5248]{1,2,0:T(8,128)(2,1)} %stack.3), calls=%async_computation.1 | async-start | bytes 42991616 | tf_op jit(solution)/shard_map/all_to_all | solution.py:141
  51.5 526.9 %all-gather.3.cloned.1.call-start = ((), (), s32[]{:S(2)}) async-start(), calls=%async_computation.5 | async-start | bytes 1114112 | tf_op jit(solution)/shard_map/all_gather | solution.py:26
  406.5 5.2 copy-start.6
  411.6 3.8 copy-start.1
  411.6 3.8 copy-start.7
  429.4 8.8 %copy-start = (bf16[2048,5248]{0,1:T(8,128)(2,1)}, bf16[2048,5248]{0,1:T(8,128)(2,1)S(1)}, u32[]{:S(2)}) copy-start(bf16[2048,5248]{0,1:T(8,128)(2,1)S(1)} %copy_bitcast_fusion.3) | copy-start | bytes 64487428
  429.4 5.3 copy-start.4
  438.2 2.3 copy-start.3
  547.6 239.0 %all-reduce.3.cloned.1.call-start = ((), (), s32[]{:S(2)}) async-start(), calls=%async_computation.3 | async-start | bytes 8388608 | tf_op jit(solution)/shard_map/psum | solution.py:214
  602.2 235.4 %reduce-scatter.2.cloned.1.call-start = ((), (), s32[]{:S(2)}) async-start(), calls=%async_computation.4 | async-start | bytes 2621440 | tf_op jit(solution)/shard_map/reduce_scatter | solution.py:226
  786.6 3.2 copy-start.11
  789.8 11.2 %copy-start.2 = (f32[512,2048]{1,0:T(8,128)}, f32[512,2048]{1,0:T(8,128)S(1)}, u32[]{:S(2)}) copy-start(f32[512,2048]{1,0:T(8,128)S(1)} %get-tuple-element.362) | copy-start | bytes 12582916
Sparse Core Ops, SparseCore 0:
  547.7 30.6 all-gather.2
  602.3 184.2 all-reduce.2
  808.5 29.0 reduce-scatter.1
